TPU v7x, 32 devices: a whole 2x2x4 slice. The times are simulated.
32 devices in a mesh: row: 4 (over y, core), col: 8 (over z, x).
Axes of the slice: x: 2, y: 2, z: 4, core: 2. Of those that a mesh axis runs over, the one named last changes fastest.
Arguments:
- normal: float32 [16, 4, 256, 8, 8, 256], P(None, 'row', None, None, 'col'), may hold values from -1.5 to 1.5
- panel_inverse: float32 [256, 256], replicated, as said below
- rhs: float32 [16, 4, 256, 512], P(None, 'row', None, 'col'), may hold values from -0.009765625 to 0.009765625
- shifts: float32 [4], replicated, may hold values from 16 to 128
Outputs:
- schur: float32 [16, 4, 256, 8, 8, 256], P(None, 'row', None, None, 'col')
- eliminated: float32 [16, 4, 256, 512], P(None, 'row', None, 'col')
- applied: float32 [16, 4, 256, 512], P(None, 'row', None, 'col')
Inputs may be any that keep to these rules, and one draw needn't show every extreme that they name: `panel_inverse`: lower triangular with positive diagonal entries.
All inputs are finite; a program needn't handle non-finite values.
Results may differ from a plain program's by a relative error of at most 0.000076.
Values sent between devices are 32-bit elements; how exact they have to be, the bound alone decides.
A program may use at most 256 MiB of HBM per device.

v0:
```python
import jax
import jax.numpy as jnp
from jax import lax
from jax.sharding import PartitionSpec as P

R = 128


def spread_2(value, axis, source):
    kept = jnp.where(lax.axis_index(axis) == source, value, 0).astype(value.dtype)
    return lax.psum(kept, axis)


def pick_blocks(blocks, spacing, offset):
    grouped = blocks.reshape((blocks.shape[0] // spacing, spacing) + blocks.shape[1:])
    return lax.dynamic_index_in_dim(grouped, offset, 1, keepdims=False)


def shards(normal, panel_inverse, rhs, shifts):
    high = lax.Precision.HIGHEST
    row_index = lax.axis_index("row")
    col_index = lax.axis_index("col")
    nrow = lax.axis_size("row")
    ncol = lax.axis_size("col")
    spacing = ncol // nrow
    brows, nb, bcols = (normal.shape[0], normal.shape[2], normal.shape[3])
    narrow = rhs.shape[3]
    wide = narrow * ncol
    tile = normal.reshape(brows * nb, bcols * nb)
    owner = col_index % nrow
    offset = col_index // nrow
    local_panel = jnp.dot(
        tile[:, :nb], panel_inverse.T, precision=high, preferred_element_type=jnp.float32
    )
    panel = spread_2(local_panel, "col", 0)
    chosen = pick_blocks(panel.reshape(brows, nb, nb), spacing, offset)
    crossed = spread_2(chosen, "row", owner).reshape(bcols * nb, nb)
    updated = tile - jnp.dot(panel, crossed.T, precision=high, preferred_element_type=jnp.float32)
    leading = spread_2(rhs[0, 0], "row", 0)
    first = jnp.dot(panel_inverse, leading, precision=high, preferred_element_type=jnp.float32)
    reduced = rhs.reshape(brows * nb, narrow) - jnp.dot(
        panel, first, precision=high, preferred_element_type=jnp.float32
    )
    reduced = reduced.reshape(brows, nb, narrow)
    reduced = reduced.at[0].set(jnp.where(row_index == 0, first, reduced[0]))
    spread = lax.all_gather(reduced, "col", axis=2, tiled=True)
    scales = lax.dynamic_slice_in_dim(jnp.repeat(shifts, R), col_index * narrow, narrow)
    partial_value = lax.dot_general(
        updated,
        spread.reshape(brows * nb, wide),
        (((0,), (0,)), ((), ())),
        precision=high,
        preferred_element_type=jnp.float32,
    )
    totals = lax.psum(partial_value, "row")
    totals = totals.reshape(bcols, nb, ncol, narrow)
    arrived = lax.all_to_all(totals, "col", split_axis=2, concat_axis=2, tiled=True)
    arrived = arrived.reshape(bcols, nb, spacing, nrow, narrow)
    arrived = lax.dynamic_index_in_dim(arrived, row_index, 3, keepdims=False)
    product = jnp.transpose(arrived, (0, 2, 1, 3)).reshape(brows, nb, narrow)
    applied = product + reduced * scales[None, None, :]
    schur = updated.reshape(brows, 1, nb, bcols, 1, nb)
    return (schur, reduced.reshape(brows, 1, nb, narrow), applied.reshape(brows, 1, nb, narrow))


def solution(mesh):
    in_specs = (P(None, "row", None, None, "col", None), P(), P(None, "row", None, "col"), P())
    out_specs = (
        P(None, "row", None, None, "col", None),
        P(None, "row", None, "col"),
        P(None, "row", None, "col"),
    )
    return jax.shard_map(shards, mesh=mesh, in_specs=in_specs, out_specs=out_specs, check_vma=False)
```

profile of v0, /device:TPU:0, one launch (start us, length us, event | category | flops | bytes accessed | tf_op | source)
XLA Modules:
  0.0 758.9 jit_solution(6350466244515718778)
XLA Ops:
  7.2 93.9 %reduce.2 = f32[16,256,8,256]{3,2,1,0:T(8,128)} reduce(f32[16,1,256,8,1,256]{5,4,3,2,1,0:T(1,128)} %param.6, f32[]{:T(128)} %constant.77), dimensions={1,4}, to_apply=%param.6.reduce_sub_computation | reduce | bytes 67108864 | tf_op args[0]
  101.1 29.9 %copy.37 = f32[512,8,8,256]{3,1,2,0:T(8,128)} copy(f32[512,8,8,256]{3,2,1,0:T(8,128)} %bitcast.49) | data formatting | bytes 67108864
  131.1 7.7 %convolution_select_fusion = f32[4096,256]{1,0:T(8,128)} fusion(f32[256,256]{1,0:T(8,128)S(1)} %copy-done, f32[4096,2048]{1,0:T(8,128)} %bitcast.47, pred[]{:T(512)S(6)} %eq.12), kind=kOutput, calls=%fused_computation.1 | convolution fusion | flops 3222274048 | bytes 8650753 | tf_op jit(solution)/shard_map/dot_general | solution.py:32
  138.8 1.1 copy-done.5
  140.6 157.4 %all-reduce.5.cloned.1.call-done = f32[4096,256]{1,0:T(8,128)} async-done(((f32[4096,256]{1,0:T(8,128)}), f32[4096,256]{1,0:T(8,128)}) %all-reduce.5.cloned.1.call-update) | async-done | bytes 4194320 | tf_op jit(solution)/shard_map/psum | solution.py:11
  298.0 3.1 dynamic-slice_select_fusion
  301.7 51.0 %all-reduce.9.cloned.1.call-done = (f32[2048,256]{1,0:T(8,128)}, f32[256,64]{0,1:T(8,128)}) async-done(((f32[2048,256]{1,0:T(8,128)}, f32[256,64]{0,1:T(8,128)}), (f32[2048,256]{1,0:T(8,128)}, f32[256,64]{0,1:T(8,128)})) %all-reduce.9.cloned.1.call-update) | async-done | bytes 2162704 | tf_op jit(solution)/shard_map/psum | solution.py:11
  352.7 1.2 fusion.3
  354.0 6.5 convolution_subtract_fusion.1
  360.9 0.9 scatter.4
  361.8 1.0 copy-done.2
  362.9 34.1 %convolution_subtract_fusion = f32[4096,2048]{1,0:T(8,128)} fusion(f32[4096,2048]{1,0:T(8,128)} %bitcast.48, f32[4096,256]{1,0:T(8,128)} %all-reduce.5.cloned.1.call-done, f32[2048,256]{1,0:T(8,128)S(1)} %copy-done.4), kind=kOutput, calls=%fused_computation | convolution fusion | flops 25778192384 | bytes 73400320 | tf_op jit(solution)/shard_map/dot_general | solution.py:38
  397.0 90.5 %all-gather.2.cloned.1.call-done = f32[16,256,512]{1,0,2:T(8,128)} async-done(((f32[16,256,64]{1,0,2:T(8,128)}), f32[16,256,512]{1,0,2:T(8,128)}) %all-gather.2.cloned.1.call-update) | async-done | bytes 8388624 | tf_op jit(solution)/shard_map/all_gather | solution.py:46
  487.5 9.9 %copy.28 = f32[16,256,512]{2,1,0:T(8,128)} copy(f32[16,256,512]{1,0,2:T(8,128)} %all-gather.2.cloned.1.call-done) | data formatting | bytes 16777216 | tf_op jit(solution)/shard_map/all_gather | solution.py:46
  497.4 64.5 %fusion.4 = f32[2048,512]{0,1:T(8,128)S(1)} fusion(f32[4096,2048]{1,0:T(8,128)} %convolution_subtract_fusion, f32[4096,512]{1,0:T(8,128)} %bitcast.55), kind=kOutput, calls=%fused_computation.13 | convolution fusion | flops 51539607552 | bytes 46137344 | tf_op jit(solution)/shard_map/dot_general | solution.py:48
  561.9 4.0 copy.40
  565.9 83.8 %all-reduce.7.cloned.1.call-done = f32[8,256,8,64]{1,0,3,2:T(8,128)} async-done(((f32[8,256,8,64]{1,0,3,2:T(8,128)}), f32[8,256,8,64]{1,0,3,2:T(8,128)}) %all-reduce.7.cloned.1.call-update) | async-done | bytes 4194320 | tf_op jit(solution)/shard_map/psum | solution.py:55
  649.7 5.5 all-to-all-start
  655.4 48.4 %reshape.98 = f32[16,1,256,8,1,256]{5,4,3,2,1,0:T(1,128)} reshape(f32[4096,2048]{1,0:T(8,128)} %convolution_subtract_fusion) | data formatting | bytes 67108864 | tf_op jit(solution)/shard_map/reshape | solution.py:62
  703.8 1.6 copy.33
  705.4 42.8 %all-to-all-done = f32[8,256,8,64]{1,0,3,2:T(8,128)} async-done(((f32[8,256,8,64]{1,0,3,2:T(8,128)}), f32[8,256,8,64]{1,0,3,2:T(8,128)}, u32[]{:S(2)}, u32[]{:S(2)}) %all-to-all-start) | async-done | bytes 4194336 | tf_op jit(solution)/shard_map/all_to_all | solution.py:57
  748.2 1.3 constant_dynamic-slice_fusion
  749.9 0.7 fusion.1
  750.6 1.6 copy.34
  (28 shorter events, 2.3 us)
Async XLA Ops:
  7.2 123.9 %copy-start = (f32[256,256]{1,0:T(8,128)S(1)}, f32[256,256]{1,0:T(8,128)}, u32[]{:S(2)}) copy-start(f32[256,256]{1,0:T(8,128)} %param.7) | copy-start | bytes 786436
  7.2 290.8 %all-reduce.5.cloned.1.call-start = ((), (), s32[]{:S(2)}) async-start(), calls=%async_computation.1 | async-start | bytes 8388608 | tf_op jit(solution)/shard_map/psum | solution.py:11
  138.7 1.2 copy-start.5
  138.7 214.0 %all-reduce.9.cloned.1.call-start = ((), (), s32[]{:S(2)}) async-start(), calls=%async_computation.4 | async-start | bytes 4325376 | tf_op jit(solution)/shard_map/psum | solution.py:11
  301.1 186.4 %all-gather.2.cloned.1.call-start = ((), (), s32[]{:S(2)}) async-start(), calls=%async_computation.2 | async-start | bytes 9437184 | tf_op jit(solution)/shard_map/all_gather | solution.py:46
  354.0 8.9 %copy-start.4 = (f32[2048,256]{1,0:T(8,128)S(1)}, f32[2048,256]{1,0:T(8,128)}, u32[]{:S(2)}) copy-start(f32[2048,256]{1,0:T(8,128)} %get-tuple-element.27) | copy-start | bytes 6291460
  361.8 1.0 copy-start.2
  362.8 286.9 %all-reduce.7.cloned.1.call-start = ((), (), s32[]{:S(2)}) async-start(), calls=%async_computation.3 | async-start | bytes 8388608 | tf_op jit(solution)/shard_map/psum | solution.py:55
  565.9 89.3 %copy-start.6 = (f32[4]{0:T(128)S(1)}, f32[4]{0:T(128)}, u32[]{:S(2)}) copy-start(f32[4]{0:T(128)} %param.9) | copy-start | bytes 52
  649.7 98.5 %all-to-all-start = ((f32[8,256,8,64]{1,0,3,2:T(8,128)}), f32[8,256,8,64]{1,0,3,2:T(8,128)}, u32[]{:S(2)}, u32[]{:S(2)}) async-start(f32[8,256,8,64]{1,0,3,2:T(8,128)} %all-reduce.7.cloned.1.call-done), calls=%async_computation | async-start | bytes 8388608 | tf_op jit(solution)/shard_map/all_to_all | solution.py:57
  655.4 48.4 %copy-start.3 = (f32[16,256,64]{1,0,2:T(8,128)S(1)}, f32[16,256,64]{1,0,2:T(8,128)}, u32[]{:S(2)}) copy-start(f32[16,256,64]{1,0,2:T(8,128)} %copy-done.2) | copy-start | bytes 3145732
  748.2 3.9 copy-start.1
Sparse Core Ops, SparseCore 0:
  138.9 159.0 all-reduce.4
  301.2 51.4 all-reduce.8
  362.9 124.5 all-gather.1
  566.0 83.6 all-reduce.6
where the time goes:
time: 768 us; the launch traced here: 759 us
  waiting for transfers between devices  426 us (55%)
  matrix products  114 us (15%)
  local copies, waits for them, and re-layouts  101 us (13%)
  other arithmetic  98.3 us (13%)
  between operations  14.1 us (2%)
    psum x2, waiting for transfers between devices, spread_2(): return lax.psum(kept, axis)  208 us
    unnamed x1, other arithmetic  93.9 us
    all_gather x1, waiting for transfers between devices, shards(): spread = lax.all_gather(reduced, 'col', axis=2, tiled=True)  90.5 us
    psum x1, waiting for transfers between devices, shards(): totals = lax.psum(partial_value, 'row')  83.8 us
    dot_general x1, matrix products, shards(): lax.dot_general(updated, spread.reshape(brows * nb, wide), (((0,), (0,)),...  64.5 us
    reshape x1, local copies, waits for them, and re-layouts, shards(): schur = updated.reshape(brows, 1, nb, bcols, 1, nb)  48.4 us
    all_to_all x1, waiting for transfers between devices, shards(): lax.all_to_all(totals, 'col', split_axis=2, concat_axis=2, tiled=True)  42.8 us
    unnamed x21, local copies, waits for them, and re-layouts  39.9 us
  transfers between devices with their start and end apart: 5, of which 5 were waited for; matrix products, arithmetic and copies ran while one was open for 11% of the time, Pallas kernels for 0%

commit v1 on v0

--- a/solution.py
+++ b/solution.py
@@ -2,8 +2,23 @@
 import jax.numpy as jnp
 from jax import lax
 from jax.sharding import PartitionSpec as P
+from jax.lax import ppermute, psum
 
 R = 128
+
+
+def feed_region(block_here):
+    nd = psum(1, axis_name="row")
+    field_out = block_here
+    for i in [hop_no for hop_no in (1, 2, 4, 8, 16) if hop_no < nd]:
+        chunks = []
+        dd = 0
+        while dd < nd:
+            chunks.append((dd, dd ^ i))
+            dd += 1
+        found_now = ppermute(field_out, axis_name="row", perm=chunks)
+        field_out = field_out + found_now
+    return field_out
 
 
 def spread_2(value, axis, source):
@@ -52,7 +67,7 @@
         precision=high,
         preferred_element_type=jnp.float32,
     )
-    totals = lax.psum(partial_value, "row")
+    totals = feed_region(partial_value)
     totals = totals.reshape(bcols, nb, ncol, narrow)
     arrived = lax.all_to_all(totals, "col", split_axis=2, concat_axis=2, tiled=True)
     arrived = arrived.reshape(bcols, nb, spacing, nrow, narrow)

time: 768 us -> 792 us (1.031)
  waiting for transfers between devices: 426 us -> 440 us
    ppermute x0 -> x2, waiting for transfers between devices: none -> 98.3 us  [feed_region(): found_now = ppermute(field_out, axis_name='row', perm=chunks)]
    psum x1 -> x0, waiting for transfers between devices: 83.8 us -> none  [shards(): totals = lax.psum(partial_value, 'row')]
  transfers between devices with their start and end apart: 5 -> 6, of which waited for: 5 -> 6; matrix products, arithmetic and copies ran while one was open for 11% -> 11% of each run, Pallas kernels for 0% -> 0%
where the time goes in v1:
time: 792 us; the launch traced here: 783 us
  waiting for transfers between devices  440 us (56%)
  matrix products  112 us (14%)
  local copies, waits for them, and re-layouts  108 us (14%)
  other arithmetic  102 us (13%)
  between operations  14.1 us (2%)
    psum x2, waiting for transfers between devices, spread_2(): return lax.psum(kept, axis)  208 us
    ppermute x2, waiting for transfers between devices, feed_region(): found_now = ppermute(field_out, axis_name='row', perm=chunks)  98.3 us
    unnamed x1, other arithmetic  93.9 us
    all_gather x1, waiting for transfers between devices, shards(): spread = lax.all_gather(reduced, 'col', axis=2, tiled=True)  90.6 us
    dot_general x1, matrix products, shards(): lax.dot_general(updated, spread.reshape(brows * nb, wide), (((0,), (0,)),...  62.1 us
    reshape x1, local copies, waits for them, and re-layouts, shards(): schur = updated.reshape(brows, 1, nb, bcols, 1, nb)  48.4 us
    all_to_all x1, waiting for transfers between devices, shards(): lax.all_to_all(totals, 'col', split_axis=2, concat_axis=2, tiled=True)  42.7 us
    unnamed x21, local copies, waits for them, and re-layouts  42 us
  transfers between devices with their start and end apart: 6, of which 6 were waited for; matrix products, arithmetic and copies ran while one was open for 11% of the time, Pallas kernels for 0%

profile of v1, /device:TPU:0, one launch (start us, length us, event | category | flops | bytes accessed | tf_op | source)
XLA Modules:
  0.0 783.2 jit_solution(12326741344457682523)
XLA Ops:
  7.2 93.9 %reduce.2 = f32[16,256,8,256]{3,2,1,0:T(8,128)} reduce(f32[16,1,256,8,1,256]{5,4,3,2,1,0:T(1,128)} %param.6, f32[]{:T(128)} %constant.77), dimensions={1,4}, to_apply=%param.6.reduce_sub_computation | reduce | bytes 67108864 | tf_op args[0]
  101.1 29.9 %copy.36 = f32[512,8,8,256]{3,1,2,0:T(8,128)} copy(f32[512,8,8,256]{3,2,1,0:T(8,128)} %bitcast.49) | data formatting | bytes 67108864
  131.1 7.7 convolution_select_fusion
  140.6 157.4 %all-reduce.4.cloned.1.call-done = f32[4096,256]{1,0:T(8,128)} async-done(((f32[4096,256]{1,0:T(8,128)}), f32[4096,256]{1,0:T(8,128)}) %all-reduce.4.cloned.1.call-update) | async-done | bytes 4194320 | tf_op jit(solution)/shard_map/psum | solution.py:26
  298.0 3.1 dynamic-slice_select_fusion
  301.8 51.0 %all-reduce.6.cloned.1.call-done = (f32[2048,256]{1,0:T(8,128)}, f32[256,64]{0,1:T(8,128)}) async-done(((f32[2048,256]{1,0:T(8,128)}, f32[256,64]{0,1:T(8,128)}), (f32[2048,256]{1,0:T(8,128)}, f32[256,64]{0,1:T(8,128)})) %all-reduce.6.cloned.1.call-update) | async-done | bytes 2162704 | tf_op jit(solution)/shard_map/psum | solution.py:26
  352.8 1.2 fusion.3
  354.0 6.5 convolution_subtract_fusion.1
  362.8 34.1 %convolution_subtract_fusion = f32[4096,2048]{1,0:T(8,128)} fusion(f32[4096,2048]{1,0:T(8,128)} %bitcast.48, f32[4096,256]{1,0:T(8,128)} %all-reduce.4.cloned.1.call-done, f32[2048,256]{1,0:T(8,128)S(1)} %copy-done.4), kind=kOutput, calls=%fused_computation | convolution fusion | flops 25778192384 | bytes 73400320 | tf_op jit(solution)/shard_map/dot_general | solution.py:53
  396.9 90.6 %all-gather.2.cloned.1.call-done = f32[16,256,512]{1,0,2:T(8,128)} async-done(((f32[16,256,64]{1,0,2:T(8,128)}), f32[16,256,512]{1,0,2:T(8,128)}) %all-gather.2.cloned.1.call-update) | async-done | bytes 8388624 | tf_op jit(solution)/shard_map/all_gather | solution.py:61
  487.5 9.9 %copy.28 = f32[16,256,512]{2,1,0:T(8,128)} copy(f32[16,256,512]{1,0,2:T(8,128)} %all-gather.2.cloned.1.call-done) | data formatting | bytes 16777216 | tf_op jit(solution)/shard_map/all_gather | solution.py:61
  497.4 62.1 %fusion.4 = f32[2048,512]{1,0:T(8,128)S(1)} fusion(f32[4096,2048]{1,0:T(8,128)} %convolution_subtract_fusion, f32[4096,512]{1,0:T(8,128)} %bitcast.56), kind=kOutput, calls=%fused_computation.13 | convolution fusion | flops 51539607552 | bytes 46137344 | tf_op jit(solution)/shard_map/dot_general | solution.py:63
  559.6 7.1 collective-permute-done
  567.7 1.5 collective-permute-start.1
  569.3 91.1 %collective-permute-done.1 = f32[2048,512]{1,0:T(8,128)S(1)} collective-permute-done((f32[2048,512]{1,0:T(8,128)S(1)}, f32[2048,512]{1,0:T(8,128)S(1)}, u32[]{:S(2)}, u32[]{:S(2)}) %collective-permute-start.1) | collective-permute-done | bytes 4194336 | tf_op jit(solution)/shard_map/ppermute | solution.py:19
  660.4 3.0 add.36
  663.5 5.4 copy.29
  668.9 6.1 copy.39
  675.0 4.7 all-to-all-start
  679.8 48.4 %reshape.98 = f32[16,1,256,8,1,256]{5,4,3,2,1,0:T(1,128)} reshape(f32[4096,2048]{1,0:T(8,128)} %convolution_subtract_fusion) | data formatting | bytes 67108864 | tf_op jit(solution)/shard_map/reshape | solution.py:77
  728.2 1.6 copy.33
  729.8 42.7 %all-to-all-done = f32[8,256,8,64]{1,0,3,2:T(8,128)} async-done(((f32[8,256,8,64]{1,0,3,2:T(8,128)}), f32[8,256,8,64]{1,0,3,2:T(8,128)}, u32[]{:S(2)}, u32[]{:S(2)}) %all-to-all-start) | async-done | bytes 4194336 | tf_op jit(solution)/shard_map/all_to_all | solution.py:72
  772.5 1.3 constant_dynamic-slice_fusion
  774.9 1.6 copy.34
  (32 shorter events, 7.0 us)
Async XLA Ops:
  7.2 123.9 %copy-start = (f32[256,256]{1,0:T(8,128)S(1)}, f32[256,256]{1,0:T(8,128)}, u32[]{:S(2)}) copy-start(f32[256,256]{1,0:T(8,128)} %param.7) | copy-start | bytes 786436
  7.2 290.8 %all-reduce.4.cloned.1.call-start = ((), (), s32[]{:S(2)}) async-start(), calls=%async_computation.1 | async-start | bytes 8388608 | tf_op jit(solution)/shard_map/psum | solution.py:26
  138.7 1.2 copy-start.5
  138.7 214.0 %all-reduce.6.cloned.1.call-start = ((), (), s32[]{:S(2)}) async-start(), calls=%async_computation.3 | async-start | bytes 4325376 | tf_op jit(solution)/shard_map/psum | solution.py:26
  301.1 186.4 %all-gather.2.cloned.1.call-start = ((), (), s32[]{:S(2)}) async-start(), calls=%async_computation.2 | async-start | bytes 9437184 | tf_op jit(solution)/shard_map/all_gather | solution.py:61
  354.0 8.8 %copy-start.4 = (f32[2048,256]{1,0:T(8,128)S(1)}, f32[2048,256]{1,0:T(8,128)}, u32[]{:S(2)}) copy-start(f32[2048,256]{1,0:T(8,128)} %get-tuple-element.27) | copy-start | bytes 6291460
  361.8 1.0 copy-start.2
  559.5 7.2 collective-permute-start
  567.7 92.7 %collective-permute-start.1 = (f32[2048,512]{1,0:T(8,128)S(1)}, f32[2048,512]{1,0:T(8,128)S(1)}, u32[]{:S(2)}, u32[]{:S(2)}) collective-permute-start(f32[2048,512]{1,0:T(8,128)S(1)} %add.35), channel_id=1, source_target_pairs={{0,16},{8,24},{16,0},{24,8},{1,17},{9,25},{17,1},{25,9},{2,18},{10... | collective-permute-start | bytes 12582920 | tf_op jit(solution)/shard_map/ppermute | solution.py:19
  675.0 4.7 copy-start.6
  675.0 97.6 %all-to-all-start = ((f32[8,256,8,64]{1,0,3,2:T(8,128)}), f32[8,256,8,64]{1,0,3,2:T(8,128)}, u32[]{:S(2)}, u32[]{:S(2)}) async-start(f32[8,256,8,64]{1,0,3,2:T(8,128)} %bitcast.51), calls=%async_computation | async-start | bytes 8388608 | tf_op jit(solution)/shard_map/all_to_all | solution.py:72
  679.8 48.4 %copy-start.3 = (f32[16,256,64]{1,0,2:T(8,128)S(1)}, f32[16,256,64]{1,0,2:T(8,128)}, u32[]{:S(2)}) copy-start(f32[16,256,64]{1,0,2:T(8,128)} %copy-done.2) | copy-start | bytes 3145732
  772.5 3.9 copy-start.1
Sparse Core Ops, SparseCore 0:
  138.9 159.1 all-reduce.3
  301.3 51.4 all-reduce.5
  362.9 124.5 all-gather.1
